TPU v7x, 32 devices: a whole 2x2x4 slice. The times are simulated.
32 devices in a mesh: sub: 8 (over y, x, core), grp: 4 (over z).
Axes of the slice: x: 2, y: 2, z: 4, core: 2. Of those that a mesh axis runs over, the one named last changes fastest.
Arguments:
- res_inner: bfloat16 [2048, 16, 144], P(('sub', 'grp')), may hold values from -6 to 6
- res_face: bfloat16 [1024, 16, 144], P(('sub', 'grp')), may hold values from -6 to 6
- inner_inv: bfloat16 [2048, 144, 144], P(('sub', 'grp')), may hold values from -0.5 to 0.5
- face_coupling: bfloat16 [1024, 144, 144], P(('sub', 'grp')), may hold values from -0.5 to 0.5
- face_elem: int32 [32, 32], P(('sub', 'grp')), may hold values from 0 to 63
- face_inv: bfloat16 [1024, 144, 144], P(('sub', 'grp')), may hold values from -0.5 to 0.5
- coarse_basis: bfloat16 [1024, 64, 144], P(('sub', 'grp')), may hold values from -0.0625 to 0.0625
- coarse_map: int32 [32, 64], P(('sub', 'grp')), may hold values from 0 to 511
- coarse_inv: float32 [512, 512], P('grp'), as said below
- recv_index: int32 [32, 32], P(('sub', 'grp')), may hold values from 0 to 8, as said below
- sharers: int32 [32, 32], P(('sub', 'grp')), may hold values from 0 to 32, as said below
Outputs:
- inner_out: bfloat16 [2048, 16, 144], P(('sub', 'grp'))
- face_out: bfloat16 [1024, 16, 144], P(('sub', 'grp'))
Inputs may be any that keep to these rules, and one draw needn't show every extreme that they name: `recv_index`: row o gives, for each subdomain s at position s, the index among the 8 blocks owned by subdomain o that slot o of subdomain s refers to, or 8 where that slot is unused. `sharers`: for a used slot, the number of used slots of all subdomains that refer to the same owned block, up to all 32 of them, which some block reaches; 0 exactly for unused slots. coarse_inv is symmetric.
All inputs are finite; a program needn't handle non-finite values.
Results may differ from a plain program's by a relative error of at most 0.006.
Values may be sent and summed in bfloat16 or wider, within the bound.
No kernel may reach another device: no remote copies, remote signals or barrier semaphores. Data moves between devices by JAX's collectives and lax.ppermute only.
A program may use at most 128 MiB of HBM per device.

v0:
```python
import jax
import jax.numpy as jnp
from jax import lax
from jax.sharding import PartitionSpec as P


def send_out(partials):
    return lax.all_to_all(partials, ("sub", "grp"), split_axis=0, concat_axis=0, tiled=True)


def send_back(spread):
    return lax.all_to_all(spread, ("sub", "grp"), split_axis=0, concat_axis=0, tiled=True)


def body(
    res_inner,
    res_face,
    inner_inv,
    face_coupling,
    face_elem,
    face_inv,
    coarse_basis,
    coarse_map,
    coarse_inv,
    recv_index,
    sharers,
):
    num_faces = res_face.shape[0]
    num_owned = num_faces // 4
    elements = res_inner.shape[0]
    num_coarse = coarse_inv.shape[1]
    counts = sharers[0]
    weights = jnp.where(counts > 0, 1.0 / jnp.maximum(counts, 1).astype(jnp.float32), 0.0)
    owner_onehot = (
        recv_index[0][None, :] == jnp.arange(num_owned, dtype=jnp.int32)[:, None]
    ).astype(jnp.bfloat16)

    def assemble(partials):
        received = send_out(partials)
        flattened = received.reshape(num_faces, -1)
        owner_sum = jnp.dot(owner_onehot, flattened, preferred_element_type=jnp.float32).astype(
            jnp.bfloat16
        )
        spread = jnp.einsum(
            "of,ok->fk", owner_onehot, owner_sum, preferred_element_type=jnp.float32
        ).astype(jnp.bfloat16)
        return send_back(spread.reshape(partials.shape))

    inner_w = jnp.einsum(
        "erb,ecb->erc", res_inner, inner_inv, preferred_element_type=jnp.float32
    ).astype(jnp.bfloat16)
    nearby = inner_w[face_elem[0]]
    condensed = res_face.astype(jnp.float32) - jnp.einsum(
        "lrb,lcb->lrc", nearby, face_coupling, preferred_element_type=jnp.float32
    )
    sent = (weights[:, None, None] * condensed).astype(jnp.bfloat16)
    gathered = assemble(sent)
    restricted = (weights[:, None, None] * gathered.astype(jnp.float32)).astype(jnp.bfloat16)
    local_coarse = jnp.einsum(
        "ljb,lrb->jr", coarse_basis, restricted, preferred_element_type=jnp.float32
    )
    coarse_onehot = (
        coarse_map[0][None, :] == jnp.arange(num_coarse, dtype=jnp.int32)[:, None]
    ).astype(jnp.float32)
    partial_rhs = jnp.dot(coarse_onehot, local_coarse, precision=lax.Precision.HIGHEST)
    coarse_rhs = lax.psum(partial_rhs, ("sub", "grp"))
    row_part = jnp.dot(coarse_inv, coarse_rhs, precision=lax.Precision.HIGHEST)
    coarse_sol = lax.all_gather(row_part, "grp", axis=0, tiled=True)
    picked = jnp.einsum(
        "kj,kr->jr", coarse_onehot, coarse_sol, precision=lax.Precision.HIGHEST
    ).astype(jnp.bfloat16)
    coarse_part = jnp.einsum(
        "ljb,jr->lrb", coarse_basis, picked, preferred_element_type=jnp.float32
    )
    local_part = jnp.einsum(
        "lrb,lcb->lrc", restricted, face_inv, preferred_element_type=jnp.float32
    )
    weighted = (weights[:, None, None] * (coarse_part + local_part)).astype(jnp.bfloat16)
    face_out = assemble(weighted)
    contrib = jnp.einsum(
        "lrc,lcb->lrb", face_out, face_coupling, preferred_element_type=jnp.float32
    )
    elem_onehot = (face_elem[0][None, :] == jnp.arange(elements, dtype=jnp.int32)[:, None]).astype(
        jnp.float32
    )
    scattered = jnp.dot(
        elem_onehot, contrib.reshape(num_faces, -1), precision=lax.Precision.HIGHEST
    ).reshape(res_inner.shape)
    inner_rhs = (res_inner.astype(jnp.float32) - scattered).astype(jnp.bfloat16)
    inner_out = jnp.einsum(
        "erb,ecb->erc", inner_rhs, inner_inv, preferred_element_type=jnp.float32
    ).astype(jnp.bfloat16)
    return (inner_out, face_out)


def solution(mesh):
    return jax.shard_map(
        body,
        mesh=mesh,
        in_specs=(
            P(("sub", "grp"), None, None),
            P(("sub", "grp"), None, None),
            P(("sub", "grp"), None, None),
            P(("sub", "grp"), None, None),
            P(("sub", "grp"), None),
            P(("sub", "grp"), None, None),
            P(("sub", "grp"), None, None),
            P(("sub", "grp"), None),
            P("grp", None),
            P(("sub", "grp"), None),
            P(("sub", "grp"), None),
        ),
        out_specs=(P(("sub", "grp"), None, None), P(("sub", "grp"), None, None)),
        check_vma=False,
    )
```

profile of v0, /device:TPU:0, one launch (start us, length us, event | category | flops | bytes accessed | tf_op | source)
XLA Modules:
  0.0 140.8 jit_solution(13594599169915256372)
XLA Ops:
  0.6 0.0 copy-start
  0.6 0.8 fusion.20
  1.5 0.0 copy-start.5
  1.5 0.7 fusion.19
  2.1 3.8 %convolution_convert_fusion.5 = bf16[64,16,144]{2,1,0:T(8,128)(2,1)S(1)} fusion(bf16[64,16,144]{2,1,0:T(8,128)(2,1)} %param.11, bf16[64,144,144]{2,1,0:T(8,128)(2,1)} %param.13), kind=kOutput, calls=%fused_computation.6 | convolution fusion | flops 42614784 | bytes 3244032 | tf_op jit(solution)/shard_map/erb,ecb->erc/dot_general | solution.py:49
  6.0 1.3 gather_fusion
  7.2 0.0 copy-done.5
  7.2 0.0 copy-done
  7.3 0.0 copy-start.1
  7.3 1.8 %fusion.2 = bf16[32,16,144]{2,1,0:T(8,128)(2,1)S(1)} fusion(bf16[32,16,144]{2,1,0:T(8,128)(2,1)} %gather_fusion, bf16[32,144,144]{2,1,0:T(8,128)(2,1)S(1)} %copy-done, bf16[32,16,144]{2,1,0:T(8,128)(2,1)} %param.12, f32[32]{0:T(128)S(1)} %fusion.20), kind=kOutput, calls=%fused_computation.12 | convolution fusion | flops 21528576 | bytes 1769600 | tf_op jit(solution)/shard_map/lrb,lcb->lrc/dot_general | solution.py:53
  9.1 17.5 %all_to_all.20 = bf16[32,16,144]{2,1,0:T(8,128)(2,1)} all-to-all(bf16[32,16,144]{2,1,0:T(8,128)(2,1)S(1)} %fusion.2), channel_id=1, replica_groups=mesh['sub'=8,'grp'=4] {'sub','grp'}, dimensions={0} | all-to-all | bytes 294912 | tf_op jit(solution)/shard_map/all_to_all | solution.py:8
  26.6 1.3 reshape.70
  27.9 1.7 %convolution_convert_fusion.1 = bf16[32,2304]{1,0:T(8,128)(2,1)} fusion(bf16[32,2304]{1,0:T(8,128)(2,1)S(1)} %reshape.70, s32[32]{0:T(128)} %bitcast.41), kind=kOutput, calls=%fused_computation.2 | convolution fusion | flops 2451968 | bytes 295040 | tf_op jit(solution)/shard_map/of,ok->fk/dot_general | solution.py:44
  29.5 0.0 copy-start.7
  29.5 2.0 %reshape.71 = bf16[32,16,144]{2,1,0:T(8,128)(2,1)} reshape(bf16[32,2304]{1,0:T(8,128)(2,1)} %convolution_convert_fusion.1) | data formatting | bytes 294912 | tf_op jit(solution)/shard_map/reshape | solution.py:47
  31.6 0.0 copy-start.6
  31.6 12.9 %all_to_all.21 = bf16[32,16,144]{2,1,0:T(8,128)(2,1)S(1)} all-to-all(bf16[32,16,144]{2,1,0:T(8,128)(2,1)} %reshape.71), channel_id=1, replica_groups=mesh['sub'=8,'grp'=4] {'sub','grp'}, dimensions={0} | all-to-all | bytes 294912 | tf_op jit(solution)/shard_map/all_to_all | solution.py:12
  44.5 0.0 copy-start.2
  44.5 0.7 copy-done.2
  45.2 0.0 copy-done.1
  45.2 1.1 convolution_bitcast_fusion.1
  46.3 1.6 %fusion.9 = f32[512,16]{1,0:T(8,128)} fusion(f32[16,64]{1,0:T(8,128)S(1)} %convolution_bitcast_fusion.1, s32[64]{0:T(128)} %bitcast.43), kind=kOutput, calls=%fused_computation.24 | convolution fusion | flops 6324224 | bytes 37120 | tf_op jit(solution)/shard_map/dot_general | solution.py:65
  47.9 41.1 %psum.7 = f32[512,16]{1,0:T(8,128)} all-reduce(f32[512,16]{1,0:T(8,128)} %fusion.9), channel_id=1, replica_groups=mesh['sub'=8,'grp'=4] {'sub','grp'}, use_global_device_ids=true, to_apply=%region_0.1 | all-reduce | flops 8192 | bytes 65536 | tf_op jit(solution)/shard_map/psum | solution.py:66
  89.0 0.0 copy-start.3
  89.0 1.6 %convolution_bitcast_fusion.2 = f32[128,16]{0,1:T(8,128)S(1)} fusion(f32[512,16]{1,0:T(8,128)} %psum.7, f32[128,512]{1,0:T(8,128)} %param.19), kind=kOutput, calls=%fused_computation.15 | convolution fusion | flops 12582912 | bytes 303104 | tf_op jit(solution)/shard_map/dot_general | solution.py:67
  90.7 13.1 %all_gather.3 = f32[512,16]{0,1:T(8,128)S(1)} all-gather(f32[128,16]{0,1:T(8,128)S(1)} %convolution_bitcast_fusion.2), channel_id=1, replica_groups=mesh['sub'=8,'grp'=4] {'grp'}, dimensions={0}, use_global_device_ids=true | all-gather | bytes 40960 | tf_op jit(solution)/shard_map/all_gather | solution.py:68
  103.8 0.0 copy-done.7
  103.8 0.2 fusion.4
  104.0 0.3 convolution_bitcast_fusion
  104.3 0.0 copy-done.6
  104.3 0.0 copy-done.3
  104.3 0.0 copy-start.4
  104.3 2.4 %fusion.3 = bf16[32,16,144]{2,1,0:T(8,128)(2,1)S(1)} fusion(f32[32,16,144]{2,1,0:T(8,128)S(1)} %convolution_bitcast_fusion, bf16[32,144,144]{2,1,0:T(8,128)(2,1)} %param.16, f32[32]{0:T(128)S(1)} %copy-done.6, bf16[32,16,144]{2,1,0:T(8,128)(2,1)S(1)} %copy-done.3), kind=kOutput, calls=%fused_computation.13 | convolution fusion | flops 21676032 | bytes 1917056 | tf_op jit(solution)/shard_map/lrb,lcb->lrc/dot_general | solution.py:75
  106.7 13.0 %all_to_all.22 = bf16[32,16,144]{2,1,0:T(8,128)(2,1)S(1)} all-to-all(bf16[32,16,144]{2,1,0:T(8,128)(2,1)S(1)} %fusion.3), channel_id=1, replica_groups=mesh['sub'=8,'grp'=4] {'sub','grp'}, dimensions={0} | all-to-all | bytes 294912 | tf_op jit(solution)/shard_map/all_to_all | solution.py:8
  119.7 0.3 reshape.72
  120.0 0.0 copy-done.4
  120.0 0.3 convolution_convert_fusion
  120.3 0.4 reshape.73
  120.7 12.7 %all_to_all.23 = bf16[32,16,144]{2,1,0:T(8,128)(2,1)S(1)} all-to-all(bf16[32,16,144]{2,1,0:T(8,128)(2,1)S(1)} %reshape.73), channel_id=1, replica_groups=mesh['sub'=8,'grp'=4] {'sub','grp'}, dimensions={0} | all-to-all | bytes 294912 | tf_op jit(solution)/shard_map/all_to_all | solution.py:12
  133.4 0.0 copy-start.8
  133.4 0.4 fusion.21
  133.8 0.3 reshape.74
  134.1 0.4 dot_general.66
  134.5 0.0 copy-done.8
  134.5 0.9 fusion.7
  135.4 4.7 %convolution_convert_fusion.4 = bf16[64,16,144]{2,1,0:T(8,128)(2,1)} fusion(bf16[64,144,144]{2,1,0:T(8,128)(2,1)} %param.13, f32[64,16,144]{2,0,1:T(8,128)S(1)} %fusion.7, bf16[64,16,144]{2,1,0:T(8,128)(2,1)} %param.11), kind=kOutput, calls=%fused_computation.5 | convolution fusion | flops 43057152 | bytes 3833856 | tf_op jit(solution)/shard_map/erb,ecb->erc/dot_general | solution.py:90
  140.1 0.7 copy.22
  (1 shorter events, 0.0 us)
Async XLA Ops:
  0.6 6.6 %copy-start = (bf16[32,144,144]{2,1,0:T(8,128)(2,1)S(1)}, bf16[32,144,144]{2,1,0:T(8,128)(2,1)}, u32[]{:S(2)}) copy-start(bf16[32,144,144]{2,1,0:T(8,128)(2,1)} %param.14) | copy-start | bytes 3981316
  1.5 5.8 %copy-start.5 = (f32[32]{0:T(128)}, f32[32]{0:T(128)S(1)}, u32[]{:S(2)}) copy-start(f32[32]{0:T(128)S(1)} %fusion.20) | copy-start | bytes 388
  7.3 38.0 %copy-start.1 = (bf16[32,64,144]{2,1,0:T(8,128)(2,1)S(1)}, bf16[32,64,144]{2,1,0:T(8,128)(2,1)}, u32[]{:S(2)}) copy-start(bf16[32,64,144]{2,1,0:T(8,128)(2,1)} %param.17) | copy-start | bytes 1769476
  29.5 74.3 %copy-start.7 = (s32[1,64]{1,0:T(1,128)S(1)}, s32[1,64]{1,0:T(1,128)}, u32[]{:S(2)}) copy-start(s32[1,64]{1,0:T(1,128)} %param.18) | copy-start | bytes 772
  31.6 72.7 %copy-start.6 = (f32[32]{0:T(128)S(1)}, f32[32]{0:T(128)}, u32[]{:S(2)}) copy-start(f32[32]{0:T(128)} %copy-done.5) | copy-start | bytes 388
  44.5 0.7 copy-start.2
  89.0 15.2 %copy-start.3 = (bf16[32,16,144]{2,1,0:T(8,128)(2,1)S(1)}, bf16[32,16,144]{2,1,0:T(8,128)(2,1)}, u32[]{:S(2)}) copy-start(bf16[32,16,144]{2,1,0:T(8,128)(2,1)} %copy-done.2) | copy-start | bytes 442372
  104.3 15.7 %copy-start.4 = (s32[1,32]{1,0:T(1,128)S(1)}, s32[1,32]{1,0:T(1,128)}, u32[]{:S(2)}) copy-start(s32[1,32]{1,0:T(1,128)} %param.20) | copy-start | bytes 388
  133.4 1.1 copy-start.8
where the time goes:
time: 141 us
  blocking collectives  110 us (78%)
  matrix products  20.8 us (15%)
  local copies, waits for them, and re-layouts  7.45 us (5%)
  other arithmetic  1.48 us (1%)
    psum x1, blocking collectives, body(): coarse_rhs = lax.psum(partial_rhs, ('sub', 'grp'))  41.1 us
    all_to_all x2, blocking collectives, send_out(): lax.all_to_all(partials, ('sub', 'grp'), split_axis=0, concat_axis=0, til...  30.4 us
    all_to_all x2, blocking collectives, send_back(): lax.all_to_all(spread, ('sub', 'grp'), split_axis=0, concat_axis=0, tiled...  25.6 us
    all_gather x1, blocking collectives, body(): coarse_sol = lax.all_gather(row_part, 'grp', axis=0, tiled=True)  13.1 us
    dot_general x1, matrix products, body(): jnp.einsum('erb,ecb->erc', inner_rhs, inner_inv, preferred_element_type=j...  4.68 us
    dot_general x1, matrix products, body(): jnp.einsum('erb,ecb->erc', res_inner, inner_inv, preferred_element_type=j...  3.82 us

commit v1 on v0

--- a/solution.py
+++ b/solution.py
@@ -2,6 +2,7 @@
 import jax.numpy as jnp
 from jax import lax
 from jax.sharding import PartitionSpec as P
+from jax.lax import axis_index, axis_size, ppermute
 
 
 def send_out(partials):
@@ -65,7 +66,14 @@
     partial_rhs = jnp.dot(coarse_onehot, local_coarse, precision=lax.Precision.HIGHEST)
     coarse_rhs = lax.psum(partial_rhs, ("sub", "grp"))
     row_part = jnp.dot(coarse_inv, coarse_rhs, precision=lax.Precision.HIGHEST)
-    coarse_sol = lax.all_gather(row_part, "grp", axis=0, tiled=True)
+    state_next, row_out = (axis_size("grp"), axis_index("grp"))
+    coarse_sol, opened = (row_part, 1)
+    while opened < state_next:
+        fresh = ppermute(coarse_sol, "grp", [(d, d ^ opened) for d in range(state_next)])
+        v1 = jnp.concatenate([coarse_sol, fresh], axis=0)
+        odd = jnp.concatenate([fresh, coarse_sol], axis=0)
+        coarse_sol = jnp.where(row_out & opened == 0, v1, odd)
+        opened = 2 * opened
     picked = jnp.einsum(
         "kj,kr->jr", coarse_onehot, coarse_sol, precision=lax.Precision.HIGHEST
     ).astype(jnp.bfloat16)

time: 141 us -> 137 us (0.972)
  blocking collectives: 110 us -> 97.3 us
  waiting for transfers between devices: 0 us -> 5.34 us
  starting transfers between devices: 0 us -> 2.97 us
    all_gather x1 -> x0, blocking collectives: 13.1 us -> none  [body(): coarse_sol = lax.all_gather(row_part, 'grp', axis=0, tiled=True)]
    ppermute x0 -> x2, waiting for transfers between devices: none -> 5.34 us  [body(): ppermute(coarse_sol, 'grp', [(d, d ^ opened) for d in range(state_next)])]
    ppermute x0 -> x2, starting transfers between devices: none -> 2.97 us  [body(): ppermute(coarse_sol, 'grp', [(d, d ^ opened) for d in range(state_next)])]
  transfers between devices with their start and end apart: 0 -> 2, of which waited for: 0 -> 2; matrix products, arithmetic and copies ran while one was open for 0% -> 0% of each run, Pallas kernels for 0% -> 0%
where the time goes in v1:
time: 137 us; the launch traced here: 136 us
  blocking collectives  97.3 us (71%)
  matrix products  20.9 us (15%)
  local copies, waits for them, and re-layouts  7.45 us (5%)
  waiting for transfers between devices  5.34 us (4%)
  starting transfers between devices  2.97 us (2%)
  other arithmetic  1.49 us (1%)
    psum x1, blocking collectives, body(): coarse_rhs = lax.psum(partial_rhs, ('sub', 'grp'))  41.1 us
    all_to_all x2, blocking collectives, send_out(): lax.all_to_all(partials, ('sub', 'grp'), split_axis=0, concat_axis=0, til...  30.5 us
    all_to_all x2, blocking collectives, send_back(): lax.all_to_all(spread, ('sub', 'grp'), split_axis=0, concat_axis=0, tiled...  25.6 us
    ppermute x2, waiting for transfers between devices, body(): ppermute(coarse_sol, 'grp', [(d, d ^ opened) for d in range(state_next)])  5.34 us
    dot_general x1, matrix products, body(): jnp.einsum('erb,ecb->erc', inner_rhs, inner_inv, preferred_element_type=j...  4.68 us
    dot_general x1, matrix products, body(): jnp.einsum('erb,ecb->erc', res_inner, inner_inv, preferred_element_type=j...  3.82 us
    ppermute x2, starting transfers between devices, body(): ppermute(coarse_sol, 'grp', [(d, d ^ opened) for d in range(state_next)])  2.97 us
  transfers between devices with their start and end apart: 2, of which 2 were waited for; matrix products, arithmetic and copies ran while one was open for 0% of the time, Pallas kernels for 0%

profile of v1, /device:TPU:0, one launch (start us, length us, event | category | flops | bytes accessed | tf_op | source)
XLA Modules:
  0.0 136.1 jit_solution(17147260302834455358)
XLA Ops:
  0.6 0.0 copy-start
  0.6 0.8 fusion.26
  1.5 0.0 copy-start.4
  1.5 0.7 fusion.25
  2.1 3.8 %convolution_convert_fusion.5 = bf16[64,16,144]{2,1,0:T(8,128)(2,1)S(1)} fusion(bf16[64,16,144]{2,1,0:T(8,128)(2,1)} %param.11, bf16[64,144,144]{2,1,0:T(8,128)(2,1)} %param.13), kind=kOutput, calls=%fused_computation.6 | convolution fusion | flops 42614784 | bytes 3244032 | tf_op jit(solution)/shard_map/erb,ecb->erc/dot_general | solution.py:50
  6.0 1.3 gather_fusion
  7.2 0.0 copy-done.4
  7.2 0.0 copy-done
  7.3 0.0 copy-start.1
  7.3 1.8 %fusion.2 = bf16[32,16,144]{2,1,0:T(8,128)(2,1)S(1)} fusion(bf16[32,16,144]{2,1,0:T(8,128)(2,1)} %gather_fusion, bf16[32,144,144]{2,1,0:T(8,128)(2,1)S(1)} %copy-done, bf16[32,16,144]{2,1,0:T(8,128)(2,1)} %param.12, f32[32]{0:T(128)S(1)} %fusion.26), kind=kOutput, calls=%fused_computation.12 | convolution fusion | flops 21528576 | bytes 1769600 | tf_op jit(solution)/shard_map/lrb,lcb->lrc/dot_general | solution.py:54
  9.1 17.5 %all_to_all.20 = bf16[32,16,144]{2,1,0:T(8,128)(2,1)} all-to-all(bf16[32,16,144]{2,1,0:T(8,128)(2,1)S(1)} %fusion.2), channel_id=1, replica_groups=mesh['sub'=8,'grp'=4] {'sub','grp'}, dimensions={0} | all-to-all | bytes 294912 | tf_op jit(solution)/shard_map/all_to_all | solution.py:9
  26.6 1.3 reshape.70
  27.9 1.7 %convolution_convert_fusion.1 = bf16[32,2304]{1,0:T(8,128)(2,1)} fusion(bf16[32,2304]{1,0:T(8,128)(2,1)S(1)} %reshape.70, s32[32]{0:T(128)} %bitcast.40), kind=kOutput, calls=%fused_computation.2 | convolution fusion | flops 2451968 | bytes 295040 | tf_op jit(solution)/shard_map/of,ok->fk/dot_general | solution.py:45
  29.5 0.0 copy-start.6
  29.5 2.0 %reshape.71 = bf16[32,16,144]{2,1,0:T(8,128)(2,1)} reshape(bf16[32,2304]{1,0:T(8,128)(2,1)} %convolution_convert_fusion.1) | data formatting | bytes 294912 | tf_op jit(solution)/shard_map/reshape | solution.py:48
  31.6 0.0 copy-start.5
  31.6 12.9 %all_to_all.21 = bf16[32,16,144]{2,1,0:T(8,128)(2,1)S(1)} all-to-all(bf16[32,16,144]{2,1,0:T(8,128)(2,1)} %reshape.71), channel_id=1, replica_groups=mesh['sub'=8,'grp'=4] {'sub','grp'}, dimensions={0} | all-to-all | bytes 294912 | tf_op jit(solution)/shard_map/all_to_all | solution.py:13
  44.5 0.0 copy-start.2
  44.5 0.7 copy-done.2
  45.2 0.0 copy-done.1
  45.2 1.1 convolution_bitcast_fusion.1
  46.3 1.6 %fusion.9 = f32[512,16]{1,0:T(8,128)} fusion(f32[16,64]{1,0:T(8,128)S(1)} %convolution_bitcast_fusion.1, s32[64]{0:T(128)} %bitcast.42), kind=kOutput, calls=%fused_computation.24 | convolution fusion | flops 6324224 | bytes 37120 | tf_op jit(solution)/shard_map/dot_general | solution.py:66
  47.9 41.1 %psum.7 = f32[512,16]{1,0:T(8,128)} all-reduce(f32[512,16]{1,0:T(8,128)} %fusion.9), channel_id=1, replica_groups=mesh['sub'=8,'grp'=4] {'sub','grp'}, use_global_device_ids=true, to_apply=%region_0.1 | all-reduce | flops 8192 | bytes 65536 | tf_op jit(solution)/shard_map/psum | solution.py:67
  89.1 1.6 %convolution_bitcast_fusion.2 = f32[128,16]{0,1:T(8,128)S(1)} fusion(f32[512,16]{1,0:T(8,128)} %psum.7, f32[128,512]{1,0:T(8,128)} %param.19), kind=kOutput, calls=%fused_computation.15 | convolution fusion | flops 12582912 | bytes 303104 | tf_op jit(solution)/shard_map/dot_general | solution.py:68
  90.7 1.3 collective-permute-start
  92.0 2.4 %collective-permute-done = f32[128,16]{0,1:T(8,128)S(1)} collective-permute-done((f32[128,16]{0,1:T(8,128)S(1)}, f32[128,16]{0,1:T(8,128)S(1)}, u32[]{:S(2)}, u32[]{:S(2)}) %collective-permute-start) | collective-permute-done | bytes 8224 | tf_op jit(solution)/shard_map/ppermute | solution.py:72
  94.3 1.7 %collective-permute-start.1 = (f32[256,16]{0,1:T(8,128)S(1)}, f32[256,16]{0,1:T(8,128)S(1)}, u32[]{:S(2)}, u32[]{:S(2)}) collective-permute-start(f32[256,16]{0,1:T(8,128)S(1)} %maximum_select_fusion.2), channel_id=1, source_target_pairs={{0,2},{1,3},{2,0},{3,1},{4,6},{5,7},{6,4},{7,5},{8,10},{9,11},{10,... | collective-permute-start | bytes 49160 | tf_op jit(solution)/shard_map/ppermute | solution.py:72
  96.0 3.0 %collective-permute-done.1 = f32[256,16]{0,1:T(8,128)S(1)} collective-permute-done((f32[256,16]{0,1:T(8,128)S(1)}, f32[256,16]{0,1:T(8,128)S(1)}, u32[]{:S(2)}, u32[]{:S(2)}) %collective-permute-start.1) | collective-permute-done | bytes 16416 | tf_op jit(solution)/shard_map/ppermute | solution.py:72
  99.0 0.0 copy-done.6
  99.0 0.2 fusion.4
  99.2 0.3 convolution_bitcast_fusion
  99.4 0.0 copy-done.5
  99.4 0.0 copy-start.3
  99.5 2.5 %fusion.3 = bf16[32,16,144]{2,1,0:T(8,128)(2,1)S(1)} fusion(f32[32,16,144]{2,1,0:T(8,128)S(1)} %convolution_bitcast_fusion, bf16[32,144,144]{2,1,0:T(8,128)(2,1)} %param.16, f32[32]{0:T(128)S(1)} %copy-done.5, bf16[32,16,144]{2,1,0:T(8,128)(2,1)} %copy-done.2), kind=kOutput, calls=%fused_computation.13 | convolution fusion | flops 21676032 | bytes 1917056 | tf_op jit(solution)/shard_map/lrb,lcb->lrc/dot_general | solution.py:83
  102.0 13.0 %all_to_all.22 = bf16[32,16,144]{2,1,0:T(8,128)(2,1)S(1)} all-to-all(bf16[32,16,144]{2,1,0:T(8,128)(2,1)S(1)} %fusion.3), channel_id=1, replica_groups=mesh['sub'=8,'grp'=4] {'sub','grp'}, dimensions={0} | all-to-all | bytes 294912 | tf_op jit(solution)/shard_map/all_to_all | solution.py:9
  115.0 0.3 reshape.72
  115.3 0.0 copy-done.3
  115.3 0.3 convolution_convert_fusion
  115.6 0.4 reshape.73
  116.1 12.7 %all_to_all.23 = bf16[32,16,144]{2,1,0:T(8,128)(2,1)S(1)} all-to-all(bf16[32,16,144]{2,1,0:T(8,128)(2,1)S(1)} %reshape.73), channel_id=1, replica_groups=mesh['sub'=8,'grp'=4] {'sub','grp'}, dimensions={0} | all-to-all | bytes 294912 | tf_op jit(solution)/shard_map/all_to_all | solution.py:13
  128.8 0.0 copy-start.7
  128.8 0.4 fusion.28
  129.2 0.3 reshape.74
  129.4 0.4 dot_general.66
  129.8 0.0 copy-done.7
  129.8 0.9 fusion.7
  130.8 4.7 %convolution_convert_fusion.4 = bf16[64,16,144]{2,1,0:T(8,128)(2,1)} fusion(bf16[64,144,144]{2,1,0:T(8,128)(2,1)} %param.13, f32[64,16,144]{2,0,1:T(8,128)S(1)} %fusion.7, bf16[64,16,144]{2,1,0:T(8,128)(2,1)} %param.11), kind=kOutput, calls=%fused_computation.5 | convolution fusion | flops 43057152 | bytes 3833856 | tf_op jit(solution)/shard_map/erb,ecb->erc/dot_general | solution.py:98
  135.4 0.7 copy.22
  (2 shorter events, 0.0 us)
Async XLA Ops:
  0.6 6.6 %copy-start = (bf16[32,144,144]{2,1,0:T(8,128)(2,1)S(1)}, bf16[32,144,144]{2,1,0:T(8,128)(2,1)}, u32[]{:S(2)}) copy-start(bf16[32,144,144]{2,1,0:T(8,128)(2,1)} %param.14) | copy-start | bytes 3981316
  1.5 5.8 %copy-start.4 = (f32[32]{0:T(128)}, f32[32]{0:T(128)S(1)}, u32[]{:S(2)}) copy-start(f32[32]{0:T(128)S(1)} %fusion.26) | copy-start | bytes 388
  7.3 38.0 %copy-start.1 = (bf16[32,64,144]{2,1,0:T(8,128)(2,1)S(1)}, bf16[32,64,144]{2,1,0:T(8,128)(2,1)}, u32[]{:S(2)}) copy-start(bf16[32,64,144]{2,1,0:T(8,128)(2,1)} %param.17) | copy-start | bytes 1769476
  29.5 69.4 %copy-start.6 = (s32[1,64]{1,0:T(1,128)S(1)}, s32[1,64]{1,0:T(1,128)}, u32[]{:S(2)}) copy-start(s32[1,64]{1,0:T(1,128)} %param.18) | copy-start | bytes 772
  31.6 67.9 %copy-start.5 = (f32[32]{0:T(128)S(1)}, f32[32]{0:T(128)}, u32[]{:S(2)}) copy-start(f32[32]{0:T(128)} %copy-done.4) | copy-start | bytes 388
  44.5 0.7 copy-start.2
  90.7 3.7 %collective-permute-start = (f32[128,16]{0,1:T(8,128)S(1)}, f32[128,16]{0,1:T(8,128)S(1)}, u32[]{:S(2)}, u32[]{:S(2)}) collective-permute-start(f32[128,16]{0,1:T(8,128)S(1)} %convolution_bitcast_fusion.2), channel_id=1, source_target_pairs={{0,1},{1,0},{2,3},{3,2},{4,5},{5,4},{6,7},{7,6},{8,9},{9,8},{10,11... | collective-permute-start | bytes 24584 | tf_op jit(solution)/shard_map/ppermute | solution.py:72
  94.3 4.6 %collective-permute-start.1 = (f32[256,16]{0,1:T(8,128)S(1)}, f32[256,16]{0,1:T(8,128)S(1)}, u32[]{:S(2)}, u32[]{:S(2)}) collective-permute-start(f32[256,16]{0,1:T(8,128)S(1)} %maximum_select_fusion.2), channel_id=1, source_target_pairs={{0,2},{1,3},{2,0},{3,1},{4,6},{5,7},{6,4},{7,5},{8,10},{9,11},{10,... | collective-permute-start | bytes 49160 | tf_op jit(solution)/shard_map/ppermute | solution.py:72
  99.4 15.9 %copy-start.3 = (s32[1,32]{1,0:T(1,128)S(1)}, s32[1,32]{1,0:T(1,128)}, u32[]{:S(2)}) copy-start(s32[1,32]{1,0:T(1,128)} %param.20) | copy-start | bytes 388
  128.8 1.1 copy-start.7
